TPU v7x, 512 devices: a whole 4x4x16 slice. The times are simulated.
512 devices in a mesh: blk: 8 (over x, core), team: 64 (over y, z).
Axes of the slice: x: 4, y: 4, z: 16, core: 2. Of those that a mesh axis runs over, the one named last changes fastest.
Arguments:
- queries: bfloat16 [8, 1024, 512], P('blk', 'team'), may hold values from -6 to 6
- keys: bfloat16 [8, 64, 256, 512], P('blk', 'team'), may hold values from -6 to 6
- values: bfloat16 [8, 64, 256, 512], P('blk', 'team'), may hold values from -40 to 40
- block_ids: int32 [8, 64, 8, 8], P('blk', 'team'), may hold values from 0 to 15, as said below
- masks: int32 [8, 64, 8, 8, 16, 128], P('blk', 'team'), may hold values from 0 to 255
- gate_input: bfloat16 [8, 1024, 512], P('blk', 'team'), may hold values from -6 to 6
- w_gate: bfloat16 [512, 512], replicated, may hold values from -0.25 to 0.25
Outputs:
- gated: bfloat16 [8, 1024, 512], P('blk', 'team')
Inputs may be any that keep to these rules, and one draw needn't show every extreme that they name: `block_ids`: each query tile lists 8 distinct blocks of its team; block c is 128 rows starting at (c % 2) * 128 of the key owner c // 2 along blk in the same team. Bit i of masks[g, t, q, j, w, a] is the mask between query row a of tile q and key row 8 w + i of listed block j.
All inputs are finite; a program needn't handle non-finite values.
Results may differ from a plain program's by a relative error of at most 0.0049.
Values may be sent and summed in bfloat16 or wider, within the bound.
No kernel may reach another device: no remote copies, remote signals or barrier semaphores. Data moves between devices by JAX's collectives and lax.ppermute only.
A program may use at most 64 MiB of HBM per device.

v0:
```python
import math

import jax
import jax.numpy as jnp
from jax import lax
from jax.sharding import PartitionSpec as P


def unpack(packed):
    shifts = jnp.arange(8, dtype=jnp.int32)
    mask_bits = jnp.bitwise_and(jnp.right_shift(packed[..., :, None, :], shifts[:, None]), 1)
    return mask_bits.reshape(packed.shape[:-2] + (packed.shape[-2] * 8, packed.shape[-1]))


def per_device(queries, keys, values, block_ids, masks, gate_input, w_gate):
    feature_width = queries.shape[-1]
    tile_rows = masks.shape[-1]
    score_scale = 1.0 / math.sqrt(feature_width)
    block_list = block_ids[0, 0]
    mask_words = masks[0, 0]
    local_rows = queries.shape[1]
    group_queries = lax.all_gather(queries[0], "team", axis=0, tiled=True)
    group_rows = group_queries.shape[0]
    key_local = keys[0, 0]
    value_local = values[0, 0]
    key_rows = lax.all_gather(key_local, "blk", axis=0, tiled=True)
    value_rows = lax.all_gather(value_local, "blk", axis=0, tiled=True)
    piece_rows = key_rows.shape[0]
    piece_blocks = piece_rows // tile_rows
    blk_index = jnp.arange(piece_blocks, dtype=jnp.int32)
    listed = (block_list[:, :, None] == blk_index[None, None, :]).astype(jnp.int32)
    dense_words = jnp.sum(listed[:, :, :, None, None] * mask_words[:, :, None, :, :], axis=1)
    mask_bits = unpack(dense_words).transpose(1, 2, 0, 3).reshape(piece_rows, group_rows)
    scores = lax.dot_general(
        key_rows, group_queries, (((1,), (1,)), ((), ())), preferred_element_type=jnp.float32
    )
    weights = (mask_bits.astype(jnp.float32) * jax.nn.sigmoid(scores * score_scale)).astype(
        jnp.bfloat16
    )
    added = lax.dot_general(
        weights, value_rows, (((0,), (0,)), ((), ())), preferred_element_type=jnp.float32
    )
    summed = lax.psum(added, "team")
    row_start = lax.axis_index("team") * local_rows
    aggregate = lax.dynamic_slice_in_dim(summed, row_start, local_rows, 0)
    gate_pre = jnp.dot(gate_input[0], w_gate, preferred_element_type=jnp.float32)
    normed = aggregate * lax.rsqrt(jnp.mean(aggregate * aggregate, axis=-1, keepdims=True) + 1e-06)
    return (jax.nn.silu(gate_pre) * normed).astype(jnp.bfloat16)[None]


def solution(mesh):
    return jax.shard_map(
        per_device,
        mesh=mesh,
        in_specs=(
            P("blk", "team", None),
            P("blk", "team", None, None),
            P("blk", "team", None, None),
            P("blk", "team", None, None),
            P("blk", "team", None, None, None, None),
            P("blk", "team", None),
            P(),
        ),
        out_specs=P("blk", "team", None),
        check_vma=False,
    )
```

profile of v0, /device:TPU:2, one launch (start us, length us, event | category | flops | bytes accessed | tf_op | source)
XLA Modules:
  0.0 524.9 jit_solution(8105395719281079299)
XLA Ops:
  6.5 0.0 copy-start
  6.5 0.0 all-gather.9.cloned.1.call-start
  6.5 0.7 all-gather.9.cloned.1.call-update
  7.3 0.0 all-gather.11.cloned.1.call-start
  7.3 0.7 all-gather.11.cloned.1.call-update
  8.0 0.0 all-gather.7.cloned.1.call-start
  8.1 0.7 all-gather.7.cloned.1.call-update
  8.7 0.0 all-reduce.2.cloned.1.call-start
  8.8 0.8 fusion.7
  9.6 2.9 multiply_reduce_fusion
  12.5 0.6 copy.8
  13.1 0.1 shift_right_arithmetic.23
  13.2 0.5 shift_right_arithmetic.20
  13.8 4.4 and_convert_fusion
  18.2 136.4 %all-gather.9.cloned.1.call-done = bf16[1,1024,512]{2,1,0:T(8,128)(2,1)} async-done(((bf16[1,16,512]{2,1,0:T(8,128)(2,1)}), bf16[1,1024,512]{2,1,0:T(8,128)(2,1)}) %all-gather.9.cloned.1.call-update) | async-done | bytes 1048592 | tf_op jit(solution)/shard_map/all_gather | solution.py:22
  154.6 30.1 %all-gather.11.cloned.1.call-done = bf16[1,1,2048,512]{3,2,1,0:T(8,128)(2,1)} async-done(((bf16[1,1,256,512]{3,2,1,0:T(8,128)(2,1)}), bf16[1,1,2048,512]{3,2,1,0:T(8,128)(2,1)}) %all-gather.11.cloned.1.call-update) | async-done | bytes 2097168 | tf_op jit(solution)/shard_map/all_gather | solution.py:27
  184.7 35.6 %all-gather.7.cloned.1.call-done = bf16[1,1,2048,512]{3,2,1,0:T(8,128)(2,1)} async-done(((bf16[1,1,256,512]{3,2,1,0:T(8,128)(2,1)}), bf16[1,1,2048,512]{3,2,1,0:T(8,128)(2,1)}) %all-gather.7.cloned.1.call-update) | async-done | bytes 2097168 | tf_op jit(solution)/shard_map/all_gather | solution.py:26
  220.3 0.0 copy-start.1
  220.3 12.8 %fusion.1 = f32[1024,512]{1,0:T(8,128)} fusion(f32[256,8,8,128]{3,2,1,0:T(8,128)} %bitcast.34, bf16[1,1,2048,512]{3,2,1,0:T(8,128)(2,1)} %all-gather.11.cloned.1.call-done, bf16[1,1,2048,512]{3,2,1,0:T(8,128)(2,1)} %all-gather.7.cloned.1.call-done, bf16[1,1024,512]{2,1,0:T(8,128)(2,1)} %all-gather.9.cloned.1.call-done), kind=kOutput, calls=%fused_computation.4 | convolution fusion | flops 4307550208 | bytes 15728640 | tf_op jit(solution)/shard_map/dot_general | solution.py:40
  233.1 0.0 all-reduce.2.cloned.1.call-update
  233.1 282.8 %all-reduce.2.cloned.1.call-done = f32[1024,512]{1,0:T(8,128)} async-done(((f32[1024,512]{1,0:T(8,128)}), f32[1024,512]{1,0:T(8,128)}) %all-reduce.2.cloned.1.call-update) | async-done | bytes 2097168 | tf_op jit(solution)/shard_map/psum | solution.py:43
  515.9 0.9 multiply_reduce_fusion.1
  516.8 0.0 copy-done
  516.8 0.0 copy-done.1
  516.8 1.6 fusion.12
  (2 shorter events, 0.0 us)
Async XLA Ops:
  6.5 510.2 %copy-start = (bf16[512,512]{1,0:T(8,128)(2,1)S(1)}, bf16[512,512]{1,0:T(8,128)(2,1)}, u32[]{:S(2)}) copy-start(bf16[512,512]{1,0:T(8,128)(2,1)} %param.13) | copy-start | bytes 1572868
  6.5 148.1 %all-gather.9.cloned.1.call-start = ((), (), s32[]{:S(2)}) async-start(), calls=%async_computation.2 | async-start | bytes 1064960 | tf_op jit(solution)/shard_map/all_gather | solution.py:22
  7.3 177.4 %all-gather.11.cloned.1.call-start = ((), (), s32[]{:S(2)}) async-start(), calls=%async_computation.3 | async-start | bytes 2359296 | tf_op jit(solution)/shard_map/all_gather | solution.py:27
  8.0 212.3 %all-gather.7.cloned.1.call-start = ((), (), s32[]{:S(2)}) async-start(), calls=%async_computation.1 | async-start | bytes 2359296 | tf_op jit(solution)/shard_map/all_gather | solution.py:26
  8.7 507.1 %all-reduce.2.cloned.1.call-start = ((), (), s32[]{:S(2)}) async-start(), calls=%async_computation | async-start | bytes 4194304 | tf_op jit(solution)/shard_map/psum | solution.py:43
  220.3 296.5 %copy-start.1 = (bf16[1,16,512]{2,1,0:T(8,128)(2,1)S(1)}, bf16[1,16,512]{2,1,0:T(8,128)(2,1)}, u32[]{:S(2)}) copy-start(bf16[1,16,512]{2,1,0:T(8,128)(2,1)} %param.12) | copy-start | bytes 49156
Sparse Core Ops, SparseCore 0:
  10.3 144.2 all-gather.8
  156.8 27.8 all-gather.10
  186.8 33.4 all-gather.6
  233.2 282.6 all-reduce.1
where the time goes:
time: 525 us
  waiting for transfers between devices  487 us (93%)
  matrix products  14.3 us (3%)
  between operations  13.2 us (3%)
  other arithmetic  9.03 us (2%)
    psum x1, waiting for transfers between devices, per_device(): summed = lax.psum(added, 'team')  283 us
    all_gather x1, waiting for transfers between devices, per_device(): group_queries = lax.all_gather(queries[0], 'team', axis=0, tiled=True)  136 us
    all_gather x1, waiting for transfers between devices, per_device(): key_rows = lax.all_gather(key_local, 'blk', axis=0, tiled=True)  35.6 us
    all_gather x1, waiting for transfers between devices, per_device(): value_rows = lax.all_gather(value_local, 'blk', axis=0, tiled=True)  30.1 us
    dot_general x1, matrix products, per_device(): lax.dot_general(weights, value_rows, (((0,), (0,)), ((), ())), preferred_...  12.8 us
  transfers between devices with their start and end apart: 4, of which 4 were waited for; matrix products, arithmetic and copies ran while one was open for 2% of the time, Pallas kernels for 0%

commit v1 on v0

v1 whole, which is shorter than its diff:
```python
import functools
import math

import jax
import jax.numpy as jnp
from jax import lax
from jax.experimental import pallas as pl
from jax.experimental.pallas import tpu as pltpu
from jax.sharding import Mesh, PartitionSpec as P

CORES = 2
Y_SIZE = 4
VMEM_LIMIT = 24 << 20
VMEM_SPEC = pl.BlockSpec(memory_space=pltpu.VMEM)


def fetch(array, axis, size, distance):
    return lax.ppermute(array, axis, [(i, (i - distance) % size) for i in range(size)])


def tree_sum(parts):
    terms = [part.astype(jnp.float32) for part in parts]
    while len(terms) > 1:
        terms = [a + b for a, b in zip(terms[::2], terms[1::2])]
    return terms[0]


def pack_kernel(*refs):
    out_ref = refs[-1]
    for at, ref in enumerate(refs[:-1]):
        out_ref[at] = ref[...]


def pack(*arrays):
    return pl.pallas_call(
        pack_kernel,
        out_shape=jax.ShapeDtypeStruct((len(arrays), *arrays[0].shape), arrays[0].dtype),
        in_specs=[VMEM_SPEC] * len(arrays),
        out_specs=VMEM_SPEC,
        compiler_params=pltpu.CompilerParams(vmem_limit_bytes=VMEM_LIMIT),
    )(*arrays)


def attend_tile(kv, query, ids, packed_ref, tile, score_scale):
    slots, words, tile_rows = packed_ref.shape[1:]
    shifts = lax.rem(lax.broadcasted_iota(jnp.int32, (tile_rows, tile_rows), 0), 8)
    weights = []
    for slot in range(slots):
        scores = lax.dot_general(
            kv[lax.div(ids[slot], 2), lax.rem(ids[slot], 2)],
            query,
            (((1,), (1,)), ((), ())),
            preferred_element_type=jnp.float32,
        )
        packed = packed_ref[tile, slot]
        packed = jnp.broadcast_to(packed[:, None, :], (words, 8, tile_rows))
        packed = packed.reshape(words * 8, tile_rows)
        bits = jnp.bitwise_and(jnp.right_shift(packed, shifts), 1)
        sigmoid = jax.nn.sigmoid(scores * score_scale)
        weights.append(jnp.where(bits == 1, sigmoid, 0.0).astype(jnp.bfloat16))
    weights = jnp.concatenate(weights, axis=0)
    value_rows = jnp.concatenate(
        [kv[lax.div(ids[slot], 2), 2 + lax.rem(ids[slot], 2)] for slot in range(slots)], axis=0
    )
    return lax.dot_general(
        weights, value_rows, (((0,), (0,)), ((), ())), preferred_element_type=jnp.float32
    )


def attend_column(d, n_y, score_scale, ids_ref, kv, query_ref, masks_ref, out_ref):
    slots = masks_ref.shape[1]
    y_tiles = out_ref.shape[0]
    first = lax.rem(lax.axis_index("y") + d, n_y) * y_tiles
    for i in range(y_tiles):
        ids = [ids_ref[first + i, slot] for slot in range(slots)]
        added = attend_tile(kv, query_ref[i], ids, masks_ref, first + i, score_scale)
        out_ref[i] = added.astype(out_ref.dtype)


def assemble(n_x, mine, swapped, kv):
    x, core = lax.axis_index("x"), lax.axis_index("core")
    for piece in range(n_x):
        base = lax.rem(x + piece, n_x) * CORES
        kv[base + core] = mine[piece][...]
        kv[base + 1 - core] = swapped[piece]


def first_kernel(d, n_x, n_y, score_scale, ids_ref, *refs):
    mine, (swapped, query_ref, masks_ref, kv, out_ref) = refs[:n_x], refs[n_x:]
    assemble(n_x, mine, swapped, kv)
    attend_column(d, n_y, score_scale, ids_ref, kv, query_ref, masks_ref, out_ref)


def attend_cost(tiles, slots, tile_rows, width):
    return pl.CostEstimate(
        flops=4 * tiles * slots * tile_rows * tile_rows * width,
        bytes_accessed=4 << 20,
        transcendentals=tiles * slots * tile_rows * tile_rows,
    )


def attend_first(d, block_list, mine, swapped, query, masks, n_x, n_y):
    tiles, slots, _, tile_rows = masks.shape
    width = query.shape[-1]
    y_tiles = tiles // n_y
    kv_shape = (4, tile_rows, width)
    kv, added = pl.pallas_call(
        functools.partial(first_kernel, d, n_x, n_y, 1.0 / math.sqrt(width)),
        out_shape=(
            jax.ShapeDtypeStruct((n_x * CORES, *kv_shape), jnp.bfloat16),
            jax.ShapeDtypeStruct((y_tiles, tile_rows, width), jnp.bfloat16),
        ),
        in_specs=[pl.BlockSpec(memory_space=pltpu.SMEM)] + [VMEM_SPEC] * (n_x + 3),
        out_specs=(VMEM_SPEC, VMEM_SPEC),
        compiler_params=pltpu.CompilerParams(vmem_limit_bytes=VMEM_LIMIT),
        cost_estimate=attend_cost(y_tiles, slots, tile_rows, width),
    )(
        block_list,
        *[piece.reshape(kv_shape) for piece in mine],
        swapped.reshape(n_x, *kv_shape),
        query.reshape(-1, tile_rows, width),
        masks,
    )
    return kv, added.reshape(-1, width)


def attend_next(d, block_list, kv, query, masks, n_y, dtype=jnp.bfloat16):
    tiles, slots, _, tile_rows = masks.shape
    width = query.shape[-1]
    y_tiles = tiles // n_y
    return pl.pallas_call(
        functools.partial(attend_column, d, n_y, 1.0 / math.sqrt(width)),
        out_shape=jax.ShapeDtypeStruct((y_tiles, tile_rows, width), dtype),
        in_specs=[pl.BlockSpec(memory_space=pltpu.SMEM)] + [VMEM_SPEC] * 3,
        out_specs=VMEM_SPEC,
        compiler_params=pltpu.CompilerParams(vmem_limit_bytes=VMEM_LIMIT),
        cost_estimate=attend_cost(y_tiles, slots, tile_rows, width),
    )(block_list, kv, query.reshape(-1, tile_rows, width), masks).reshape(-1, width)


def per_device(n_x, n_y, n_z, queries, keys, values, block_ids, masks, gate_input, w_gate):
    block_list = block_ids[0, 0]
    mask_words = masks[0, 0]
    local_rows, width = queries.shape[1:]
    query = queries[0]
    own = jnp.concatenate([keys[0, 0], values[0, 0]], axis=0)
    along_x = []
    for d in range(1, n_x):
        along_x.append(fetch(own, "x", n_x, d))
    column = lax.all_to_all(jnp.broadcast_to(query, (n_z, *query.shape)), "z", 0, 0)
    column = column.reshape(n_z * local_rows, width)
    along_x, column = lax.optimization_barrier((along_x, column))
    mine = [own, *along_x]
    packed = pack(*mine)
    swapped = fetch(packed, "core", CORES, 1)
    columns = [column]
    for d in range(1, n_y):
        columns.append(fetch(column, "y", n_y, d))
    kv, parts = None, []
    for d in (1, 3, 2, 0):
        if kv is None:
            kv, added = attend_first(d, block_list, mine, swapped, columns[d], mask_words, n_x, n_y)
        else:
            dtype = jnp.bfloat16 if d else jnp.float32
            added = attend_next(d, block_list, kv, columns[d], mask_words, n_y, dtype)
        parts.append(fetch(added, "y", n_y, -d) if d else added)
    summed = tree_sum(parts).astype(jnp.bfloat16)
    parts = lax.all_to_all(summed.reshape(n_z, local_rows, width), "z", 0, 0)
    aggregate = tree_sum(parts)
    gate_pre = jnp.dot(gate_input[0], w_gate, preferred_element_type=jnp.float32)
    normed = aggregate * lax.rsqrt(jnp.mean(aggregate * aggregate, axis=-1, keepdims=True) + 1e-06)
    return (jax.nn.silu(gate_pre) * normed).astype(jnp.bfloat16)[None]


def solution(mesh):
    n_x, n_y = mesh.shape["blk"] // CORES, Y_SIZE
    n_z = mesh.shape["team"] // n_y
    fine = Mesh(mesh.devices.reshape(n_x, CORES, n_y, n_z), ("x", "core", "y", "z"))
    blk, team = ("x", "core"), ("y", "z")

    def program(*args):
        return per_device(n_x, n_y, n_z, *args)

    return jax.shard_map(
        program,
        mesh=fine,
        in_specs=(
            P(blk, team, None),
            P(blk, team, None, None),
            P(blk, team, None, None),
            P(blk, team, None, None),
            P(blk, team, None, None, None, None),
            P(blk, team, None),
            P(),
        ),
        out_specs=P(blk, team, None),
        check_vma=False,
    )
```

time: 525 us -> 127 us (0.24)
  the two profiles are of different devices: /device:TPU:2 before, /device:TPU:32 now
where the time goes in v1:
time: 127 us
  starting transfers between devices  46.1 us (36%)
  waiting for transfers between devices  40 us (31%)
  blocking collectives  29.4 us (23%)
  Pallas kernels  7.39 us (6%)
  local copies, waits for them, and re-layouts  1.52 us (1%)
  other arithmetic  1.38 us (1%)
    ppermute x10, waiting for transfers between devices, fetch(): lax.ppermute(array, axis, [(i, (i - distance) % size) for i in range(size)])  40 us
    ppermute x10, starting transfers between devices, fetch(): lax.ppermute(array, axis, [(i, (i - distance) % size) for i in range(size)])  30.9 us
    all_to_all x1, blocking collectives, per_device(): parts = lax.all_to_all(summed.reshape(n_z, local_rows, width), 'z', 0, 0)  29.4 us
    all_to_all x1, starting transfers between devices, per_device(): lax.all_to_all(jnp.broadcast_to(query, (n_z, *query.shape)), 'z', 0, 0)  15.2 us
    pallas_call x3, Pallas kernels, attend_next(): pl.pallas_call(functools.partial(attend_column, d, n_y, 1.0 / math.sqrt(w...  5.24 us
  transfers between devices with their start and end apart: 11, of which 6 were waited for; matrix products, arithmetic and copies ran while one was open for 1% of the time, Pallas kernels for 6%

profile of v1, /device:TPU:32, one launch (start us, length us, event | category | flops | bytes accessed | tf_op | source)
XLA Modules:
  0.0 126.8 jit_solution(2045118625746369225)
XLA Ops:
  0.0 0.0 copy-start
  0.0 1.5 %broadcast_in_dim.7 = bf16[16,16,512]{2,1,0:T(8,128)(2,1)} broadcast(bf16[16,512]{1,0:T(8,128)(2,1)} %bitcast.72), dimensions={1,2} | broadcast | bytes 278528 | tf_op jit(solution)/shard_map/broadcast_in_dim | solution.py:150
  1.5 15.2 %all-to-all-start = ((bf16[16,16,512]{2,1,0:T(8,128)(2,1)}), bf16[16,16,512]{2,1,0:T(8,128)(2,1)S(1)}, u32[]{:S(2)}, u32[]{:S(2)}) async-start(bf16[16,16,512]{2,1,0:T(8,128)(2,1)} %broadcast_in_dim.7), calls=%async_computation | async-start | bytes 524288 | tf_op jit(solution)/shard_map/all_to_all | solution.py:150
  16.7 1.1 pad_maximum_fusion.refs_0_
  17.8 4.7 %collective-permute-start = (bf16[512,512]{1,0:T(8,128)(2,1)S(1)}, bf16[512,512]{1,0:T(8,128)(2,1)S(1)}, u32[]{:S(2)}, u32[]{:S(2)}) collective-permute-start(bf16[512,512]{1,0:T(8,128)(2,1)S(1)} %pad_maximum_fusion.refs_0_), channel_id=1, source_target_pairs={{0,384},{128,0},{256,128},{384,256},{1,385},{129,1},{257,129},{385... | collective-permute-start | bytes 1572872 | tf_op jit(solution)/shard_map/ppermute | solution.py:18
  22.5 2.7 %collective-permute-start.1 = (bf16[512,512]{1,0:T(8,128)(2,1)S(1)}, bf16[512,512]{1,0:T(8,128)(2,1)S(1)}, u32[]{:S(2)}, u32[]{:S(2)}) collective-permute-start(bf16[512,512]{1,0:T(8,128)(2,1)S(1)} %pad_maximum_fusion.refs_0_), channel_id=1, source_target_pairs={{0,256},{128,384},{256,0},{384,128},{1,257},{129,385},{257,1},{385... | collective-permute-start | bytes 1572872 | tf_op jit(solution)/shard_map/ppermute | solution.py:18
  25.2 2.8 %collective-permute-start.2 = (bf16[512,512]{1,0:T(8,128)(2,1)S(1)}, bf16[512,512]{1,0:T(8,128)(2,1)S(1)}, u32[]{:S(2)}, u32[]{:S(2)}) collective-permute-start(bf16[512,512]{1,0:T(8,128)(2,1)S(1)} %pad_maximum_fusion.refs_0_), channel_id=1, source_target_pairs={{0,128},{128,256},{256,384},{384,0},{1,129},{129,257},{257,385},{3... | collective-permute-start | bytes 1572872 | tf_op jit(solution)/shard_map/ppermute | solution.py:18
  28.0 16.3 %collective-permute-done.refs_1_ = bf16[512,512]{1,0:T(8,128)(2,1)S(1)} collective-permute-done((bf16[512,512]{1,0:T(8,128)(2,1)S(1)}, bf16[512,512]{1,0:T(8,128)(2,1)S(1)}, u32[]{:S(2)}, u32[]{:S(2)}) %collective-permute-start) | collective-permute-done | bytes 524320 | tf_op jit(solution)/shard_map/ppermute | solution.py:18
  44.3 0.0 collective-permute-done.1.refs_2_
  44.3 5.6 %collective-permute-done.2.refs_3_ = bf16[512,512]{1,0:T(8,128)(2,1)S(1)} collective-permute-done((bf16[512,512]{1,0:T(8,128)(2,1)S(1)}, bf16[512,512]{1,0:T(8,128)(2,1)S(1)}, u32[]{:S(2)}, u32[]{:S(2)}) %collective-permute-start.2) | collective-permute-done | bytes 524320 | tf_op jit(solution)/shard_map/ppermute | solution.py:18
  49.9 0.0 all-to-all-done
  49.9 0.0 copy-start.1
  49.9 0.0 copy-start.2
  49.9 0.1 shard_map.73
  50.1 2.1 %collective-permute-start.3 = (bf16[4,512,512]{2,1,0:T(8,128)(2,1)S(1)}, bf16[4,512,512]{2,1,0:T(8,128)(2,1)S(1)}, u32[]{:S(2)}, u32[]{:S(2)}) collective-permute-start(bf16[4,512,512]{2,1,0:T(8,128)(2,1)S(1)} %shard_map.73), channel_id=1, source_target_pairs={{0,64},{64,0},{1,65},{65,1},{2,66},{66,2},{3,67},{67,3},{4,68},{68... | collective-permute-start | bytes 6291464 | tf_op jit(solution)/shard_map/ppermute | solution.py:18
  52.1 4.9 %collective-permute-start.4 = (bf16[256,512]{1,0:T(8,128)(2,1)S(1)}, bf16[256,512]{1,0:T(8,128)(2,1)S(1)}, u32[]{:S(2)}, u32[]{:S(2)}) collective-permute-start(bf16[256,512]{1,0:T(8,128)(2,1)S(1)} %bitcast.55), channel_id=1, source_target_pairs={{0,48},{16,0},{32,16},{48,32},{1,49},{17,1},{33,17},{49,33},{2,50}... | collective-permute-start | bytes 786440 | tf_op jit(solution)/shard_map/ppermute | solution.py:18
  57.1 1.9 %collective-permute-start.6 = (bf16[256,512]{1,0:T(8,128)(2,1)S(1)}, bf16[256,512]{1,0:T(8,128)(2,1)S(1)}, u32[]{:S(2)}, u32[]{:S(2)}) collective-permute-start(bf16[256,512]{1,0:T(8,128)(2,1)S(1)} %bitcast.56), channel_id=1, source_target_pairs={{0,16},{16,32},{32,48},{48,0},{1,17},{17,33},{33,49},{49,1},{2,18}... | collective-permute-start | bytes 786440 | tf_op jit(solution)/shard_map/ppermute | solution.py:18
  59.0 4.1 %collective-permute-start.8 = (bf16[256,512]{1,0:T(8,128)(2,1)S(1)}, bf16[256,512]{1,0:T(8,128)(2,1)S(1)}, u32[]{:S(2)}, u32[]{:S(2)}) collective-permute-start(bf16[256,512]{1,0:T(8,128)(2,1)S(1)} %bitcast.57), channel_id=1, source_target_pairs={{0,32},{16,48},{32,0},{48,16},{1,33},{17,49},{33,1},{49,17},{2,34}... | collective-permute-start | bytes 786440 | tf_op jit(solution)/shard_map/ppermute | solution.py:18
  63.1 0.2 collective-permute-done.4
  63.3 0.0 collective-permute-done.3
  63.3 0.0 copy-done.1
  63.3 0.0 copy-done.2
  63.3 2.0 %shard_map.74 = (bf16[8,4,128,512]{3,2,1,0:T(8,128)(2,1)S(1)}, bf16[2,128,512]{2,1,0:T(8,128)(2,1)S(1)}) custom-call(s32[8,8]{1,0:T(8,128)S(1)} %bitcast.64, bf16[4,128,512]{2,1,0:T(8,128)(2,1)S(1)} %bitcast.50, bf16[4,128,512]{2,1,0:T(8,128)(2,1)S(1)} %bitcast.52, bf16[4,128,512]{2,1,0:T(8,128)(2,1)S(1)} %bitcast.53, bf16[4,128,512]{2,1,0:T(8,128)(2,1)S(1)} %bitcast.54, ...), custom_call_target="tpu_custom_call" | custom-call | flops 536870912 | bytes 4194304 | tf_op jit(solution)/shard_map/pallas_call | solution.py:107
  65.3 8.9 %collective-permute-done.6 = bf16[256,512]{1,0:T(8,128)(2,1)S(1)} collective-permute-done((bf16[256,512]{1,0:T(8,128)(2,1)S(1)}, bf16[256,512]{1,0:T(8,128)(2,1)S(1)}, u32[]{:S(2)}, u32[]{:S(2)}) %collective-permute-start.6) | collective-permute-done | bytes 262176 | tf_op jit(solution)/shard_map/ppermute | solution.py:18
  74.2 1.7 %shard_map.75 = bf16[2,128,512]{2,1,0:T(8,128)(2,1)S(1)} custom-call(s32[8,8]{1,0:T(8,128)S(1)} %bitcast.65, bf16[8,4,128,512]{3,2,1,0:T(8,128)(2,1)S(1)} %get-tuple-element.16.kv, bf16[2,128,512]{2,1,0:T(8,128)(2,1)S(1)} %bitcast.60, s32[8,8,16,128]{3,2,1,0:T(8,128)S(1)} %bitcast.47), custom_call_target="tpu_custom_call" | custom-call | flops 536870912 | bytes 4194304 | tf_op jit(solution)/shard_map/pallas_call | solution.py:131
  76.0 1.9 %collective-permute-start.7 = (bf16[256,512]{1,0:T(8,128)(2,1)S(1)}, bf16[256,512]{1,0:T(8,128)(2,1)S(1)}, u32[]{:S(2)}, u32[]{:S(2)}) collective-permute-start(bf16[256,512]{1,0:T(8,128)(2,1)S(1)} %bitcast.62), channel_id=1, source_target_pairs={{0,48},{16,0},{32,16},{48,32},{1,49},{17,1},{33,17},{49,33},{2,50}... | collective-permute-start | bytes 786440 | tf_op jit(solution)/shard_map/ppermute | solution.py:18
  77.9 0.0 collective-permute-done.8
  77.9 1.8 %shard_map.76 = bf16[2,128,512]{2,1,0:T(8,128)(2,1)S(1)} custom-call(s32[8,8]{1,0:T(8,128)S(1)} %bitcast.66, bf16[8,4,128,512]{3,2,1,0:T(8,128)(2,1)S(1)} %get-tuple-element.16.kv, bf16[2,128,512]{2,1,0:T(8,128)(2,1)S(1)} %bitcast.59, s32[8,8,16,128]{3,2,1,0:T(8,128)S(1)} %bitcast.48), custom_call_target="tpu_custom_call" | custom-call | flops 536870912 | bytes 4194304 | tf_op jit(solution)/shard_map/pallas_call | solution.py:131
  79.7 1.9 %collective-permute-start.9 = (bf16[256,512]{1,0:T(8,128)(2,1)S(1)}, bf16[256,512]{1,0:T(8,128)(2,1)S(1)}, u32[]{:S(2)}, u32[]{:S(2)}) collective-permute-start(bf16[256,512]{1,0:T(8,128)(2,1)S(1)} %bitcast.63), channel_id=1, source_target_pairs={{0,32},{16,48},{32,0},{48,16},{1,33},{17,49},{33,1},{49,17},{2,34}... | collective-permute-start | bytes 786440 | tf_op jit(solution)/shard_map/ppermute | solution.py:18
  81.6 3.9 %collective-permute-start.5 = (bf16[256,512]{1,0:T(8,128)(2,1)S(1)}, bf16[256,512]{1,0:T(8,128)(2,1)S(1)}, u32[]{:S(2)}, u32[]{:S(2)}) collective-permute-start(bf16[256,512]{1,0:T(8,128)(2,1)S(1)} %bitcast.68), channel_id=1, source_target_pairs={{0,16},{16,32},{32,48},{48,0},{1,17},{17,33},{33,49},{49,1},{2,18}... | collective-permute-start | bytes 786440 | tf_op jit(solution)/shard_map/ppermute | solution.py:18
  85.5 1.8 %shard_map.77 = f32[2,128,512]{2,1,0:T(8,128)S(1)} custom-call(s32[8,8]{1,0:T(8,128)S(1)} %bitcast.67, bf16[8,4,128,512]{3,2,1,0:T(8,128)(2,1)S(1)} %get-tuple-element.16.kv, bf16[2,128,512]{2,1,0:T(8,128)(2,1)S(1)} %bitcast.58, s32[8,8,16,128]{3,2,1,0:T(8,128)S(1)} %bitcast.49), custom_call_target="tpu_custom_call" | custom-call | flops 536870912 | bytes 4194304 | tf_op jit(solution)/shard_map/pallas_call | solution.py:131
  87.3 0.0 copy-start.3
  87.3 0.0 collective-permute-done.7
  87.3 4.9 %collective-permute-done.9 = bf16[256,512]{1,0:T(8,128)(2,1)S(1)} collective-permute-done((bf16[256,512]{1,0:T(8,128)(2,1)S(1)}, bf16[256,512]{1,0:T(8,128)(2,1)S(1)}, u32[]{:S(2)}, u32[]{:S(2)}) %collective-permute-start.9) | collective-permute-done | bytes 262176 | tf_op jit(solution)/shard_map/ppermute | solution.py:18
  92.2 4.0 %collective-permute-done.5 = bf16[256,512]{1,0:T(8,128)(2,1)S(1)} collective-permute-done((bf16[256,512]{1,0:T(8,128)(2,1)S(1)}, bf16[256,512]{1,0:T(8,128)(2,1)S(1)}, u32[]{:S(2)}, u32[]{:S(2)}) %collective-permute-start.5) | collective-permute-done | bytes 262176 | tf_op jit(solution)/shard_map/ppermute | solution.py:18
  96.2 0.2 fusion.1
  96.4 29.4 %all_to_all.10 = bf16[16,16,512]{2,1,0:T(8,128)(2,1)S(1)} all-to-all(bf16[16,16,512]{2,1,0:T(8,128)(2,1)S(1)} %bitcast.69), channel_id=1, replica_groups=mesh['x'=4,'core'=2,'y'=4,'z'=16] {'z'}, dimensions={0} | all-to-all | bytes 524288 | tf_op jit(solution)/shard_map/all_to_all | solution.py:168
  125.8 0.1 fusion.2
  126.0 0.0 copy-done
  126.0 0.0 copy-done.3
  126.0 0.8 fusion.9
  (1 shorter events, 0.0 us)
Async XLA Ops:
  0.0 126.0 %copy-start = (bf16[512,512]{1,0:T(8,128)(2,1)S(1)}, bf16[512,512]{1,0:T(8,128)(2,1)}, u32[]{:S(2)}) copy-start(bf16[512,512]{1,0:T(8,128)(2,1)} %param.13) | copy-start | bytes 1572868
  1.5 48.4 %all-to-all-start = ((bf16[16,16,512]{2,1,0:T(8,128)(2,1)}), bf16[16,16,512]{2,1,0:T(8,128)(2,1)S(1)}, u32[]{:S(2)}, u32[]{:S(2)}) async-start(bf16[16,16,512]{2,1,0:T(8,128)(2,1)} %broadcast_in_dim.7), calls=%async_computation | async-start | bytes 524288 | tf_op jit(solution)/shard_map/all_to_all | solution.py:150
  17.8 26.5 %collective-permute-start = (bf16[512,512]{1,0:T(8,128)(2,1)S(1)}, bf16[512,512]{1,0:T(8,128)(2,1)S(1)}, u32[]{:S(2)}, u32[]{:S(2)}) collective-permute-start(bf16[512,512]{1,0:T(8,128)(2,1)S(1)} %pad_maximum_fusion.refs_0_), channel_id=1, source_target_pairs={{0,384},{128,0},{256,128},{384,256},{1,385},{129,1},{257,129},{385... | collective-permute-start | bytes 1572872 | tf_op jit(solution)/shard_map/ppermute | solution.py:18
  22.5 21.9 %collective-permute-start.1 = (bf16[512,512]{1,0:T(8,128)(2,1)S(1)}, bf16[512,512]{1,0:T(8,128)(2,1)S(1)}, u32[]{:S(2)}, u32[]{:S(2)}) collective-permute-start(bf16[512,512]{1,0:T(8,128)(2,1)S(1)} %pad_maximum_fusion.refs_0_), channel_id=1, source_target_pairs={{0,256},{128,384},{256,0},{384,128},{1,257},{129,385},{257,1},{385... | collective-permute-start | bytes 1572872 | tf_op jit(solution)/shard_map/ppermute | solution.py:18
  25.2 24.7 %collective-permute-start.2 = (bf16[512,512]{1,0:T(8,128)(2,1)S(1)}, bf16[512,512]{1,0:T(8,128)(2,1)S(1)}, u32[]{:S(2)}, u32[]{:S(2)}) collective-permute-start(bf16[512,512]{1,0:T(8,128)(2,1)S(1)} %pad_maximum_fusion.refs_0_), channel_id=1, source_target_pairs={{0,128},{128,256},{256,384},{384,0},{1,129},{129,257},{257,385},{3... | collective-permute-start | bytes 1572872 | tf_op jit(solution)/shard_map/ppermute | solution.py:18
  49.9 13.3 %copy-start.1 = (s32[1,1,8,8,16,128]{5,4,3,2,1,0:T(8,128)S(1)}, s32[1,1,8,8,16,128]{5,4,3,2,1,0:T(8,128)}, u32[]{:S(2)}) copy-start(s32[1,1,8,8,16,128]{5,4,3,2,1,0:T(8,128)} %param.11) | copy-start | bytes 1572868
  49.9 13.3 %copy-start.2 = (s32[1,1,8,8]{3,2,1,0:T(8,128)S(1)}, s32[1,1,8,8]{3,2,1,0:T(8,128)}, u32[]{:S(2)}) copy-start(s32[1,1,8,8]{3,2,1,0:T(8,128)} %param.10) | copy-start | bytes 772
  50.1 13.2 %collective-permute-start.3 = (bf16[4,512,512]{2,1,0:T(8,128)(2,1)S(1)}, bf16[4,512,512]{2,1,0:T(8,128)(2,1)S(1)}, u32[]{:S(2)}, u32[]{:S(2)}) collective-permute-start(bf16[4,512,512]{2,1,0:T(8,128)(2,1)S(1)} %shard_map.73), channel_id=1, source_target_pairs={{0,64},{64,0},{1,65},{65,1},{2,66},{66,2},{3,67},{67,3},{4,68},{68... | collective-permute-start | bytes 6291464 | tf_op jit(solution)/shard_map/ppermute | solution.py:18
  52.1 11.1 %collective-permute-start.4 = (bf16[256,512]{1,0:T(8,128)(2,1)S(1)}, bf16[256,512]{1,0:T(8,128)(2,1)S(1)}, u32[]{:S(2)}, u32[]{:S(2)}) collective-permute-start(bf16[256,512]{1,0:T(8,128)(2,1)S(1)} %bitcast.55), channel_id=1, source_target_pairs={{0,48},{16,0},{32,16},{48,32},{1,49},{17,1},{33,17},{49,33},{2,50}... | collective-permute-start | bytes 786440 | tf_op jit(solution)/shard_map/ppermute | solution.py:18
  57.1 17.1 %collective-permute-start.6 = (bf16[256,512]{1,0:T(8,128)(2,1)S(1)}, bf16[256,512]{1,0:T(8,128)(2,1)S(1)}, u32[]{:S(2)}, u32[]{:S(2)}) collective-permute-start(bf16[256,512]{1,0:T(8,128)(2,1)S(1)} %bitcast.56), channel_id=1, source_target_pairs={{0,16},{16,32},{32,48},{48,0},{1,17},{17,33},{33,49},{49,1},{2,18}... | collective-permute-start | bytes 786440 | tf_op jit(solution)/shard_map/ppermute | solution.py:18
  59.0 18.9 %collective-permute-start.8 = (bf16[256,512]{1,0:T(8,128)(2,1)S(1)}, bf16[256,512]{1,0:T(8,128)(2,1)S(1)}, u32[]{:S(2)}, u32[]{:S(2)}) collective-permute-start(bf16[256,512]{1,0:T(8,128)(2,1)S(1)} %bitcast.57), channel_id=1, source_target_pairs={{0,32},{16,48},{32,0},{48,16},{1,33},{17,49},{33,1},{49,17},{2,34}... | collective-permute-start | bytes 786440 | tf_op jit(solution)/shard_map/ppermute | solution.py:18
  76.0 11.3 %collective-permute-start.7 = (bf16[256,512]{1,0:T(8,128)(2,1)S(1)}, bf16[256,512]{1,0:T(8,128)(2,1)S(1)}, u32[]{:S(2)}, u32[]{:S(2)}) collective-permute-start(bf16[256,512]{1,0:T(8,128)(2,1)S(1)} %bitcast.62), channel_id=1, source_target_pairs={{0,48},{16,0},{32,16},{48,32},{1,49},{17,1},{33,17},{49,33},{2,50}... | collective-permute-start | bytes 786440 | tf_op jit(solution)/shard_map/ppermute | solution.py:18
  79.7 12.6 %collective-permute-start.9 = (bf16[256,512]{1,0:T(8,128)(2,1)S(1)}, bf16[256,512]{1,0:T(8,128)(2,1)S(1)}, u32[]{:S(2)}, u32[]{:S(2)}) collective-permute-start(bf16[256,512]{1,0:T(8,128)(2,1)S(1)} %bitcast.63), channel_id=1, source_target_pairs={{0,32},{16,48},{32,0},{48,16},{1,33},{17,49},{33,1},{49,17},{2,34}... | collective-permute-start | bytes 786440 | tf_op jit(solution)/shard_map/ppermute | solution.py:18
  81.6 14.6 %collective-permute-start.5 = (bf16[256,512]{1,0:T(8,128)(2,1)S(1)}, bf16[256,512]{1,0:T(8,128)(2,1)S(1)}, u32[]{:S(2)}, u32[]{:S(2)}) collective-permute-start(bf16[256,512]{1,0:T(8,128)(2,1)S(1)} %bitcast.68), channel_id=1, source_target_pairs={{0,16},{16,32},{32,48},{48,0},{1,17},{17,33},{33,49},{49,1},{2,18}... | collective-permute-start | bytes 786440 | tf_op jit(solution)/shard_map/ppermute | solution.py:18
  87.3 38.7 %copy-start.3 = (bf16[1,16,512]{2,1,0:T(8,128)(2,1)S(1)}, bf16[1,16,512]{2,1,0:T(8,128)(2,1)}, u32[]{:S(2)}) copy-start(bf16[1,16,512]{2,1,0:T(8,128)(2,1)} %param.12) | copy-start | bytes 49156

commit v2 on v1

--- a/solution.py
+++ b/solution.py
@@ -153,11 +153,12 @@
     mine = [own, *along_x]
     packed = pack(*mine)
     swapped = fetch(packed, "core", CORES, 1)
-    columns = [column]
-    for d in range(1, n_y):
-        columns.append(fetch(column, "y", n_y, d))
+    columns = {0: column}
+    for d in (1, n_y - 1):
+        columns[d] = fetch(column, "y", n_y, d)
+    columns[2] = fetch(column, "y", n_y, 2)
     kv, parts = None, []
-    for d in (1, 3, 2, 0):
+    for d in (2, 3, 1, 0):
         if kv is None:
             kv, added = attend_first(d, block_list, mine, swapped, columns[d], mask_words, n_x, n_y)
         else:

time: 127 us -> 125 us (0.984)
  waiting for transfers between devices: 40 us -> 33.4 us
  starting transfers between devices: 46.1 us -> 50.5 us
    ppermute x10, waiting for transfers between devices: 40 us -> 33.3 us  [fetch(): lax.ppermute(array, axis, [(i, (i - distance) % size) for i in range(size)])]
    ppermute x10, starting transfers between devices: 30.9 us -> 35.3 us  [fetch(): lax.ppermute(array, axis, [(i, (i - distance) % size) for i in range(size)])]
where the time goes in v2:
time: 125 us; the launch traced here: 124 us
  starting transfers between devices  50.5 us (40%)
  waiting for transfers between devices  33.4 us (27%)
  blocking collectives  29.3 us (23%)
  Pallas kernels  7.38 us (6%)
  local copies, waits for them, and re-layouts  1.52 us (1%)
  other arithmetic  1.38 us (1%)
    ppermute x10, starting transfers between devices, fetch(): lax.ppermute(array, axis, [(i, (i - distance) % size) for i in range(size)])  35.3 us
    ppermute x10, waiting for transfers between devices, fetch(): lax.ppermute(array, axis, [(i, (i - distance) % size) for i in range(size)])  33.3 us
    all_to_all x1, blocking collectives, per_device(): parts = lax.all_to_all(summed.reshape(n_z, local_rows, width), 'z', 0, 0)  29.3 us
    all_to_all x1, starting transfers between devices, per_device(): lax.all_to_all(jnp.broadcast_to(query, (n_z, *query.shape)), 'z', 0, 0)  15.2 us
    pallas_call x3, Pallas kernels, attend_next(): pl.pallas_call(functools.partial(attend_column, d, n_y, 1.0 / math.sqrt(w...  5.24 us
  transfers between devices with their start and end apart: 11, of which 6 were waited for; matrix products, arithmetic and copies ran while one was open for 1% of the time, Pallas kernels for 6%

profile of v2, /device:TPU:32, one launch (start us, length us, event | category | flops | bytes accessed | tf_op | source)
XLA Modules:
  0.0 124.5 jit_solution(12520302295254063655)
XLA Ops:
  0.0 0.0 copy-start
  0.0 1.5 %broadcast_in_dim.7 = bf16[16,16,512]{2,1,0:T(8,128)(2,1)} broadcast(bf16[16,512]{1,0:T(8,128)(2,1)} %bitcast.72), dimensions={1,2} | broadcast | bytes 278528 | tf_op jit(solution)/shard_map/broadcast_in_dim | solution.py:150
  1.5 15.2 %all-to-all-start = ((bf16[16,16,512]{2,1,0:T(8,128)(2,1)}), bf16[16,16,512]{2,1,0:T(8,128)(2,1)S(1)}, u32[]{:S(2)}, u32[]{:S(2)}) async-start(bf16[16,16,512]{2,1,0:T(8,128)(2,1)} %broadcast_in_dim.7), calls=%async_computation | async-start | bytes 524288 | tf_op jit(solution)/shard_map/all_to_all | solution.py:150
  16.7 1.1 pad_maximum_fusion.refs_0_
  17.8 4.7 %collective-permute-start = (bf16[512,512]{1,0:T(8,128)(2,1)S(1)}, bf16[512,512]{1,0:T(8,128)(2,1)S(1)}, u32[]{:S(2)}, u32[]{:S(2)}) collective-permute-start(bf16[512,512]{1,0:T(8,128)(2,1)S(1)} %pad_maximum_fusion.refs_0_), channel_id=1, source_target_pairs={{0,384},{128,0},{256,128},{384,256},{1,385},{129,1},{257,129},{385... | collective-permute-start | bytes 1572872 | tf_op jit(solution)/shard_map/ppermute | solution.py:18
  22.5 2.7 %collective-permute-start.1 = (bf16[512,512]{1,0:T(8,128)(2,1)S(1)}, bf16[512,512]{1,0:T(8,128)(2,1)S(1)}, u32[]{:S(2)}, u32[]{:S(2)}) collective-permute-start(bf16[512,512]{1,0:T(8,128)(2,1)S(1)} %pad_maximum_fusion.refs_0_), channel_id=1, source_target_pairs={{0,256},{128,384},{256,0},{384,128},{1,257},{129,385},{257,1},{385... | collective-permute-start | bytes 1572872 | tf_op jit(solution)/shard_map/ppermute | solution.py:18
  25.2 2.8 %collective-permute-start.2 = (bf16[512,512]{1,0:T(8,128)(2,1)S(1)}, bf16[512,512]{1,0:T(8,128)(2,1)S(1)}, u32[]{:S(2)}, u32[]{:S(2)}) collective-permute-start(bf16[512,512]{1,0:T(8,128)(2,1)S(1)} %pad_maximum_fusion.refs_0_), channel_id=1, source_target_pairs={{0,128},{128,256},{256,384},{384,0},{1,129},{129,257},{257,385},{3... | collective-permute-start | bytes 1572872 | tf_op jit(solution)/shard_map/ppermute | solution.py:18
  28.0 16.3 %collective-permute-done.refs_1_ = bf16[512,512]{1,0:T(8,128)(2,1)S(1)} collective-permute-done((bf16[512,512]{1,0:T(8,128)(2,1)S(1)}, bf16[512,512]{1,0:T(8,128)(2,1)S(1)}, u32[]{:S(2)}, u32[]{:S(2)}) %collective-permute-start) | collective-permute-done | bytes 524320 | tf_op jit(solution)/shard_map/ppermute | solution.py:18
  44.3 0.0 collective-permute-done.1.refs_2_
  44.3 5.6 %collective-permute-done.2.refs_3_ = bf16[512,512]{1,0:T(8,128)(2,1)S(1)} collective-permute-done((bf16[512,512]{1,0:T(8,128)(2,1)S(1)}, bf16[512,512]{1,0:T(8,128)(2,1)S(1)}, u32[]{:S(2)}, u32[]{:S(2)}) %collective-permute-start.2) | collective-permute-done | bytes 524320 | tf_op jit(solution)/shard_map/ppermute | solution.py:18
  49.9 0.0 all-to-all-done
  49.9 0.0 copy-start.1
  49.9 0.0 copy-start.2
  49.9 0.1 shard_map.73
  50.1 2.1 %collective-permute-start.3 = (bf16[4,512,512]{2,1,0:T(8,128)(2,1)S(1)}, bf16[4,512,512]{2,1,0:T(8,128)(2,1)S(1)}, u32[]{:S(2)}, u32[]{:S(2)}) collective-permute-start(bf16[4,512,512]{2,1,0:T(8,128)(2,1)S(1)} %shard_map.73), channel_id=1, source_target_pairs={{0,64},{64,0},{1,65},{65,1},{2,66},{66,2},{3,67},{67,3},{4,68},{68... | collective-permute-start | bytes 6291464 | tf_op jit(solution)/shard_map/ppermute | solution.py:18
  52.1 5.1 %collective-permute-start.4 = (bf16[256,512]{1,0:T(8,128)(2,1)S(1)}, bf16[256,512]{1,0:T(8,128)(2,1)S(1)}, u32[]{:S(2)}, u32[]{:S(2)}) collective-permute-start(bf16[256,512]{1,0:T(8,128)(2,1)S(1)} %bitcast.55), channel_id=1, source_target_pairs={{0,32},{16,48},{32,0},{48,16},{1,33},{17,49},{33,1},{49,17},{2,34}... | collective-permute-start | bytes 786440 | tf_op jit(solution)/shard_map/ppermute | solution.py:18
  57.2 2.6 %collective-permute-start.6 = (bf16[256,512]{1,0:T(8,128)(2,1)S(1)}, bf16[256,512]{1,0:T(8,128)(2,1)S(1)}, u32[]{:S(2)}, u32[]{:S(2)}) collective-permute-start(bf16[256,512]{1,0:T(8,128)(2,1)S(1)} %bitcast.56), channel_id=1, source_target_pairs={{0,16},{16,32},{32,48},{48,0},{1,17},{17,33},{33,49},{49,1},{2,18}... | collective-permute-start | bytes 786440 | tf_op jit(solution)/shard_map/ppermute | solution.py:18
  59.8 4.5 %collective-permute-start.8 = (bf16[256,512]{1,0:T(8,128)(2,1)S(1)}, bf16[256,512]{1,0:T(8,128)(2,1)S(1)}, u32[]{:S(2)}, u32[]{:S(2)}) collective-permute-start(bf16[256,512]{1,0:T(8,128)(2,1)S(1)} %bitcast.57), channel_id=1, source_target_pairs={{0,48},{16,0},{32,16},{48,32},{1,49},{17,1},{33,17},{49,33},{2,50}... | collective-permute-start | bytes 786440 | tf_op jit(solution)/shard_map/ppermute | solution.py:18
  64.3 0.4 collective-permute-done.4
  64.7 0.0 collective-permute-done.3
  64.7 0.0 copy-done.1
  64.7 0.0 copy-done.2
  64.7 2.0 %shard_map.74 = (bf16[8,4,128,512]{3,2,1,0:T(8,128)(2,1)S(1)}, bf16[2,128,512]{2,1,0:T(8,128)(2,1)S(1)}) custom-call(s32[8,8]{1,0:T(8,128)S(1)} %bitcast.64, bf16[4,128,512]{2,1,0:T(8,128)(2,1)S(1)} %bitcast.50, bf16[4,128,512]{2,1,0:T(8,128)(2,1)S(1)} %bitcast.52, bf16[4,128,512]{2,1,0:T(8,128)(2,1)S(1)} %bitcast.53, bf16[4,128,512]{2,1,0:T(8,128)(2,1)S(1)} %bitcast.54, ...), custom_call_target="tpu_custom_call" | custom-call | flops 536870912 | bytes 4194304 | tf_op jit(solution)/shard_map/pallas_call | solution.py:107
  66.7 3.1 %collective-permute-done.6 = bf16[256,512]{1,0:T(8,128)(2,1)S(1)} collective-permute-done((bf16[256,512]{1,0:T(8,128)(2,1)S(1)}, bf16[256,512]{1,0:T(8,128)(2,1)S(1)}, u32[]{:S(2)}, u32[]{:S(2)}) %collective-permute-start.6) | collective-permute-done | bytes 262176 | tf_op jit(solution)/shard_map/ppermute | solution.py:18
  69.8 1.7 %shard_map.75 = bf16[2,128,512]{2,1,0:T(8,128)(2,1)S(1)} custom-call(s32[8,8]{1,0:T(8,128)S(1)} %bitcast.65, bf16[8,4,128,512]{3,2,1,0:T(8,128)(2,1)S(1)} %get-tuple-element.16.kv, bf16[2,128,512]{2,1,0:T(8,128)(2,1)S(1)} %bitcast.60, s32[8,8,16,128]{3,2,1,0:T(8,128)S(1)} %bitcast.47), custom_call_target="tpu_custom_call" | custom-call | flops 536870912 | bytes 4194304 | tf_op jit(solution)/shard_map/pallas_call | solution.py:131
  71.6 2.5 %collective-permute-start.7 = (bf16[256,512]{1,0:T(8,128)(2,1)S(1)}, bf16[256,512]{1,0:T(8,128)(2,1)S(1)}, u32[]{:S(2)}, u32[]{:S(2)}) collective-permute-start(bf16[256,512]{1,0:T(8,128)(2,1)S(1)} %bitcast.62), channel_id=1, source_target_pairs={{0,48},{16,0},{32,16},{48,32},{1,49},{17,1},{33,17},{49,33},{2,50}... | collective-permute-start | bytes 786440 | tf_op jit(solution)/shard_map/ppermute | solution.py:18
  74.1 0.0 collective-permute-done.8
  74.1 1.7 %shard_map.76 = bf16[2,128,512]{2,1,0:T(8,128)(2,1)S(1)} custom-call(s32[8,8]{1,0:T(8,128)S(1)} %bitcast.66, bf16[8,4,128,512]{3,2,1,0:T(8,128)(2,1)S(1)} %get-tuple-element.16.kv, bf16[2,128,512]{2,1,0:T(8,128)(2,1)S(1)} %bitcast.59, s32[8,8,16,128]{3,2,1,0:T(8,128)S(1)} %bitcast.48), custom_call_target="tpu_custom_call" | custom-call | flops 536870912 | bytes 4194304 | tf_op jit(solution)/shard_map/pallas_call | solution.py:131
  75.8 3.4 %collective-permute-start.9 = (bf16[256,512]{1,0:T(8,128)(2,1)S(1)}, bf16[256,512]{1,0:T(8,128)(2,1)S(1)}, u32[]{:S(2)}, u32[]{:S(2)}) collective-permute-start(bf16[256,512]{1,0:T(8,128)(2,1)S(1)} %bitcast.63), channel_id=1, source_target_pairs={{0,16},{16,32},{32,48},{48,0},{1,17},{17,33},{33,49},{49,1},{2,18}... | collective-permute-start | bytes 786440 | tf_op jit(solution)/shard_map/ppermute | solution.py:18
  79.2 5.1 %collective-permute-start.5 = (bf16[256,512]{1,0:T(8,128)(2,1)S(1)}, bf16[256,512]{1,0:T(8,128)(2,1)S(1)}, u32[]{:S(2)}, u32[]{:S(2)}) collective-permute-start(bf16[256,512]{1,0:T(8,128)(2,1)S(1)} %bitcast.68), channel_id=1, source_target_pairs={{0,32},{16,48},{32,0},{48,16},{1,33},{17,49},{33,1},{49,17},{2,34}... | collective-permute-start | bytes 786440 | tf_op jit(solution)/shard_map/ppermute | solution.py:18
  84.3 1.7 %shard_map.77 = f32[2,128,512]{2,1,0:T(8,128)S(1)} custom-call(s32[8,8]{1,0:T(8,128)S(1)} %bitcast.67, bf16[8,4,128,512]{3,2,1,0:T(8,128)(2,1)S(1)} %get-tuple-element.16.kv, bf16[2,128,512]{2,1,0:T(8,128)(2,1)S(1)} %bitcast.58, s32[8,8,16,128]{3,2,1,0:T(8,128)S(1)} %bitcast.49), custom_call_target="tpu_custom_call" | custom-call | flops 536870912 | bytes 4194304 | tf_op jit(solution)/shard_map/pallas_call | solution.py:131
  86.1 0.0 copy-start.3
  86.1 0.0 collective-permute-done.7
  86.1 1.1 collective-permute-done.9
  87.2 6.8 %collective-permute-done.5 = bf16[256,512]{1,0:T(8,128)(2,1)S(1)} collective-permute-done((bf16[256,512]{1,0:T(8,128)(2,1)S(1)}, bf16[256,512]{1,0:T(8,128)(2,1)S(1)}, u32[]{:S(2)}, u32[]{:S(2)}) %collective-permute-start.5) | collective-permute-done | bytes 262176 | tf_op jit(solution)/shard_map/ppermute | solution.py:18
  94.0 0.2 fusion.1
  94.2 29.3 %all_to_all.10 = bf16[16,16,512]{2,1,0:T(8,128)(2,1)S(1)} all-to-all(bf16[16,16,512]{2,1,0:T(8,128)(2,1)S(1)} %bitcast.69), channel_id=1, replica_groups=mesh['x'=4,'core'=2,'y'=4,'z'=16] {'z'}, dimensions={0} | all-to-all | bytes 524288 | tf_op jit(solution)/shard_map/all_to_all | solution.py:169
  123.5 0.1 fusion.2
  123.6 0.0 copy-done
  123.6 0.0 copy-done.3
  123.6 0.8 fusion.9
  (1 shorter events, 0.0 us)
Async XLA Ops:
  0.0 123.6 %copy-start = (bf16[512,512]{1,0:T(8,128)(2,1)S(1)}, bf16[512,512]{1,0:T(8,128)(2,1)}, u32[]{:S(2)}) copy-start(bf16[512,512]{1,0:T(8,128)(2,1)} %param.13) | copy-start | bytes 1572868
  1.5 48.4 %all-to-all-start = ((bf16[16,16,512]{2,1,0:T(8,128)(2,1)}), bf16[16,16,512]{2,1,0:T(8,128)(2,1)S(1)}, u32[]{:S(2)}, u32[]{:S(2)}) async-start(bf16[16,16,512]{2,1,0:T(8,128)(2,1)} %broadcast_in_dim.7), calls=%async_computation | async-start | bytes 524288 | tf_op jit(solution)/shard_map/all_to_all | solution.py:150
  17.8 26.5 %collective-permute-start = (bf16[512,512]{1,0:T(8,128)(2,1)S(1)}, bf16[512,512]{1,0:T(8,128)(2,1)S(1)}, u32[]{:S(2)}, u32[]{:S(2)}) collective-permute-start(bf16[512,512]{1,0:T(8,128)(2,1)S(1)} %pad_maximum_fusion.refs_0_), channel_id=1, source_target_pairs={{0,384},{128,0},{256,128},{384,256},{1,385},{129,1},{257,129},{385... | collective-permute-start | bytes 1572872 | tf_op jit(solution)/shard_map/ppermute | solution.py:18
  22.5 21.9 %collective-permute-start.1 = (bf16[512,512]{1,0:T(8,128)(2,1)S(1)}, bf16[512,512]{1,0:T(8,128)(2,1)S(1)}, u32[]{:S(2)}, u32[]{:S(2)}) collective-permute-start(bf16[512,512]{1,0:T(8,128)(2,1)S(1)} %pad_maximum_fusion.refs_0_), channel_id=1, source_target_pairs={{0,256},{128,384},{256,0},{384,128},{1,257},{129,385},{257,1},{385... | collective-permute-start | bytes 1572872 | tf_op jit(solution)/shard_map/ppermute | solution.py:18
  25.2 24.7 %collective-permute-start.2 = (bf16[512,512]{1,0:T(8,128)(2,1)S(1)}, bf16[512,512]{1,0:T(8,128)(2,1)S(1)}, u32[]{:S(2)}, u32[]{:S(2)}) collective-permute-start(bf16[512,512]{1,0:T(8,128)(2,1)S(1)} %pad_maximum_fusion.refs_0_), channel_id=1, source_target_pairs={{0,128},{128,256},{256,384},{384,0},{1,129},{129,257},{257,385},{3... | collective-permute-start | bytes 1572872 | tf_op jit(solution)/shard_map/ppermute | solution.py:18
  49.9 14.8 %copy-start.1 = (s32[1,1,8,8,16,128]{5,4,3,2,1,0:T(8,128)S(1)}, s32[1,1,8,8,16,128]{5,4,3,2,1,0:T(8,128)}, u32[]{:S(2)}) copy-start(s32[1,1,8,8,16,128]{5,4,3,2,1,0:T(8,128)} %param.11) | copy-start | bytes 1572868
  49.9 14.8 %copy-start.2 = (s32[1,1,8,8]{3,2,1,0:T(8,128)S(1)}, s32[1,1,8,8]{3,2,1,0:T(8,128)}, u32[]{:S(2)}) copy-start(s32[1,1,8,8]{3,2,1,0:T(8,128)} %param.10) | copy-start | bytes 772
  50.1 14.6 %collective-permute-start.3 = (bf16[4,512,512]{2,1,0:T(8,128)(2,1)S(1)}, bf16[4,512,512]{2,1,0:T(8,128)(2,1)S(1)}, u32[]{:S(2)}, u32[]{:S(2)}) collective-permute-start(bf16[4,512,512]{2,1,0:T(8,128)(2,1)S(1)} %shard_map.73), channel_id=1, source_target_pairs={{0,64},{64,0},{1,65},{65,1},{2,66},{66,2},{3,67},{67,3},{4,68},{68... | collective-permute-start | bytes 6291464 | tf_op jit(solution)/shard_map/ppermute | solution.py:18
  52.1 12.6 %collective-permute-start.4 = (bf16[256,512]{1,0:T(8,128)(2,1)S(1)}, bf16[256,512]{1,0:T(8,128)(2,1)S(1)}, u32[]{:S(2)}, u32[]{:S(2)}) collective-permute-start(bf16[256,512]{1,0:T(8,128)(2,1)S(1)} %bitcast.55), channel_id=1, source_target_pairs={{0,32},{16,48},{32,0},{48,16},{1,33},{17,49},{33,1},{49,17},{2,34}... | collective-permute-start | bytes 786440 | tf_op jit(solution)/shard_map/ppermute | solution.py:18
  57.2 12.6 %collective-permute-start.6 = (bf16[256,512]{1,0:T(8,128)(2,1)S(1)}, bf16[256,512]{1,0:T(8,128)(2,1)S(1)}, u32[]{:S(2)}, u32[]{:S(2)}) collective-permute-start(bf16[256,512]{1,0:T(8,128)(2,1)S(1)} %bitcast.56), channel_id=1, source_target_pairs={{0,16},{16,32},{32,48},{48,0},{1,17},{17,33},{33,49},{49,1},{2,18}... | collective-permute-start | bytes 786440 | tf_op jit(solution)/shard_map/ppermute | solution.py:18
  59.8 14.2 %collective-permute-start.8 = (bf16[256,512]{1,0:T(8,128)(2,1)S(1)}, bf16[256,512]{1,0:T(8,128)(2,1)S(1)}, u32[]{:S(2)}, u32[]{:S(2)}) collective-permute-start(bf16[256,512]{1,0:T(8,128)(2,1)S(1)} %bitcast.57), channel_id=1, source_target_pairs={{0,48},{16,0},{32,16},{48,32},{1,49},{17,1},{33,17},{49,33},{2,50}... | collective-permute-start | bytes 786440 | tf_op jit(solution)/shard_map/ppermute | solution.py:18
  71.6 14.5 %collective-permute-start.7 = (bf16[256,512]{1,0:T(8,128)(2,1)S(1)}, bf16[256,512]{1,0:T(8,128)(2,1)S(1)}, u32[]{:S(2)}, u32[]{:S(2)}) collective-permute-start(bf16[256,512]{1,0:T(8,128)(2,1)S(1)} %bitcast.62), channel_id=1, source_target_pairs={{0,48},{16,0},{32,16},{48,32},{1,49},{17,1},{33,17},{49,33},{2,50}... | collective-permute-start | bytes 786440 | tf_op jit(solution)/shard_map/ppermute | solution.py:18
  75.8 11.4 %collective-permute-start.9 = (bf16[256,512]{1,0:T(8,128)(2,1)S(1)}, bf16[256,512]{1,0:T(8,128)(2,1)S(1)}, u32[]{:S(2)}, u32[]{:S(2)}) collective-permute-start(bf16[256,512]{1,0:T(8,128)(2,1)S(1)} %bitcast.63), channel_id=1, source_target_pairs={{0,16},{16,32},{32,48},{48,0},{1,17},{17,33},{33,49},{49,1},{2,18}... | collective-permute-start | bytes 786440 | tf_op jit(solution)/shard_map/ppermute | solution.py:18
  79.2 14.8 %collective-permute-start.5 = (bf16[256,512]{1,0:T(8,128)(2,1)S(1)}, bf16[256,512]{1,0:T(8,128)(2,1)S(1)}, u32[]{:S(2)}, u32[]{:S(2)}) collective-permute-start(bf16[256,512]{1,0:T(8,128)(2,1)S(1)} %bitcast.68), channel_id=1, source_target_pairs={{0,32},{16,48},{32,0},{48,16},{1,33},{17,49},{33,1},{49,17},{2,34}... | collective-permute-start | bytes 786440 | tf_op jit(solution)/shard_map/ppermute | solution.py:18
  86.1 37.5 %copy-start.3 = (bf16[1,16,512]{2,1,0:T(8,128)(2,1)S(1)}, bf16[1,16,512]{2,1,0:T(8,128)(2,1)}, u32[]{:S(2)}) copy-start(bf16[1,16,512]{2,1,0:T(8,128)(2,1)} %param.12) | copy-start | bytes 49156

commit v3 on v2

--- a/solution.py
+++ b/solution.py
@@ -39,6 +39,21 @@
         out_specs=VMEM_SPEC,
         compiler_params=pltpu.CompilerParams(vmem_limit_bytes=VMEM_LIMIT),
     )(*arrays)
+
+
+def gate_kernel(gate_ref, w_ref, out_ref):
+    gate_pre = jnp.dot(gate_ref[...], w_ref[...], preferred_element_type=jnp.float32)
+    out_ref[...] = jax.nn.silu(gate_pre)
+
+
+def gate(gate_input, w_gate):
+    return pl.pallas_call(
+        gate_kernel,
+        out_shape=jax.ShapeDtypeStruct(gate_input.shape, jnp.float32),
+        in_specs=[VMEM_SPEC] * 2,
+        out_specs=VMEM_SPEC,
+        compiler_params=pltpu.CompilerParams(vmem_limit_bytes=VMEM_LIMIT),
+    )(gate_input, w_gate)
 
 
 def attend_tile(kv, query, ids, packed_ref, tile, score_scale):
@@ -158,7 +173,7 @@
         columns[d] = fetch(column, "y", n_y, d)
     columns[2] = fetch(column, "y", n_y, 2)
     kv, parts = None, []
-    for d in (2, 3, 1, 0):
+    for d in (2, 1, 3, 0):
         if kv is None:
             kv, added = attend_first(d, block_list, mine, swapped, columns[d], mask_words, n_x, n_y)
         else:
@@ -168,9 +183,9 @@
     summed = tree_sum(parts).astype(jnp.bfloat16)
     parts = lax.all_to_all(summed.reshape(n_z, local_rows, width), "z", 0, 0)
     aggregate = tree_sum(parts)
-    gate_pre = jnp.dot(gate_input[0], w_gate, preferred_element_type=jnp.float32)
+    gated = gate(gate_input[0], w_gate)
     normed = aggregate * lax.rsqrt(jnp.mean(aggregate * aggregate, axis=-1, keepdims=True) + 1e-06)
-    return (jax.nn.silu(gate_pre) * normed).astype(jnp.bfloat16)[None]
+    return (gated * normed).astype(jnp.bfloat16)[None]
 
 
 def solution(mesh):

time: 125 us -> 125 us (level)
  the two profiles are of different devices: /device:TPU:32 before, /device:TPU:8 now
where the time goes in v3:
time: 125 us; the launch traced here: 124 us
  starting transfers between devices  59.3 us (47%)
  waiting for transfers between devices  53.2 us (43%)
  Pallas kernels  7.57 us (6%)
  other arithmetic  2.76 us (2%)
  local copies, waits for them, and re-layouts  1.45 us (1%)
    ppermute x10, waiting for transfers between devices, fetch(): lax.ppermute(array, axis, [(i, (i - distance) % size) for i in range(size)])  35.7 us
    ppermute x10, starting transfers between devices, fetch(): lax.ppermute(array, axis, [(i, (i - distance) % size) for i in range(size)])  32.3 us
    all_to_all x1, waiting for transfers between devices, per_device(): parts = lax.all_to_all(summed.reshape(n_z, local_rows, width), 'z', 0, 0)  17.5 us
    all_to_all x1, starting transfers between devices, per_device(): lax.all_to_all(jnp.broadcast_to(query, (n_z, *query.shape)), 'z', 0, 0)  15.2 us
    all_to_all x1, starting transfers between devices, per_device(): parts = lax.all_to_all(summed.reshape(n_z, local_rows, width), 'z', 0, 0)  11.8 us
    pallas_call x3, Pallas kernels, attend_next(): pl.pallas_call(functools.partial(attend_column, d, n_y, 1.0 / math.sqrt(w...  5.23 us
  transfers between devices with their start and end apart: 12, of which 7 were waited for; matrix products, arithmetic and copies ran while one was open for 1% of the time, Pallas kernels for 6%

profile of v3, /device:TPU:8, one launch (start us, length us, event | category | flops | bytes accessed | tf_op | source)
XLA Modules:
  0.0 124.5 jit_solution(11271946929179526797)
XLA Ops:
  0.0 1.4 %broadcast_in_dim.7 = bf16[16,16,512]{2,1,0:T(8,128)(2,1)} broadcast(bf16[16,512]{1,0:T(8,128)(2,1)} %bitcast.65), dimensions={1,2} | broadcast | bytes 278528 | tf_op jit(solution)/shard_map/broadcast_in_dim | solution.py:165
  1.4 15.2 %all-to-all-start = ((bf16[16,16,512]{2,1,0:T(8,128)(2,1)}), bf16[16,16,512]{2,1,0:T(8,128)(2,1)S(1)}, u32[]{:S(2)}, u32[]{:S(2)}) async-start(bf16[16,16,512]{2,1,0:T(8,128)(2,1)} %broadcast_in_dim.7), calls=%async_computation | async-start | bytes 524288 | tf_op jit(solution)/shard_map/all_to_all | solution.py:165
  16.6 1.1 pad_maximum_fusion.refs_0_
  17.7 4.7 %collective-permute-start = (bf16[512,512]{1,0:T(8,128)(2,1)S(1)}, bf16[512,512]{1,0:T(8,128)(2,1)S(1)}, u32[]{:S(2)}, u32[]{:S(2)}) collective-permute-start(bf16[512,512]{1,0:T(8,128)(2,1)S(1)} %pad_maximum_fusion.refs_0_), channel_id=1, source_target_pairs={{0,384},{128,0},{256,128},{384,256},{1,385},{129,1},{257,129},{385... | collective-permute-start | bytes 1572872 | tf_op jit(solution)/shard_map/ppermute | solution.py:18
  22.4 2.7 %collective-permute-start.1 = (bf16[512,512]{1,0:T(8,128)(2,1)S(1)}, bf16[512,512]{1,0:T(8,128)(2,1)S(1)}, u32[]{:S(2)}, u32[]{:S(2)}) collective-permute-start(bf16[512,512]{1,0:T(8,128)(2,1)S(1)} %pad_maximum_fusion.refs_0_), channel_id=1, source_target_pairs={{0,256},{128,384},{256,0},{384,128},{1,257},{129,385},{257,1},{385... | collective-permute-start | bytes 1572872 | tf_op jit(solution)/shard_map/ppermute | solution.py:18
  25.1 2.8 %collective-permute-start.2 = (bf16[512,512]{1,0:T(8,128)(2,1)S(1)}, bf16[512,512]{1,0:T(8,128)(2,1)S(1)}, u32[]{:S(2)}, u32[]{:S(2)}) collective-permute-start(bf16[512,512]{1,0:T(8,128)(2,1)S(1)} %pad_maximum_fusion.refs_0_), channel_id=1, source_target_pairs={{0,128},{128,256},{256,384},{384,0},{1,129},{129,257},{257,385},{3... | collective-permute-start | bytes 1572872 | tf_op jit(solution)/shard_map/ppermute | solution.py:18
  27.9 16.6 %collective-permute-done.refs_1_ = bf16[512,512]{1,0:T(8,128)(2,1)S(1)} collective-permute-done((bf16[512,512]{1,0:T(8,128)(2,1)S(1)}, bf16[512,512]{1,0:T(8,128)(2,1)S(1)}, u32[]{:S(2)}, u32[]{:S(2)}) %collective-permute-start) | collective-permute-done | bytes 524320 | tf_op jit(solution)/shard_map/ppermute | solution.py:18
  44.5 0.0 collective-permute-done.1.refs_2_
  44.5 5.6 %collective-permute-done.2.refs_3_ = bf16[512,512]{1,0:T(8,128)(2,1)S(1)} collective-permute-done((bf16[512,512]{1,0:T(8,128)(2,1)S(1)}, bf16[512,512]{1,0:T(8,128)(2,1)S(1)}, u32[]{:S(2)}, u32[]{:S(2)}) %collective-permute-start.2) | collective-permute-done | bytes 524320 | tf_op jit(solution)/shard_map/ppermute | solution.py:18
  50.1 0.0 all-to-all-done
  50.1 0.0 copy-start
  50.1 0.0 copy-start.2
  50.1 0.1 shard_map.74
  50.3 2.1 %collective-permute-start.3 = (bf16[4,512,512]{2,1,0:T(8,128)(2,1)S(1)}, bf16[4,512,512]{2,1,0:T(8,128)(2,1)S(1)}, u32[]{:S(2)}, u32[]{:S(2)}) collective-permute-start(bf16[4,512,512]{2,1,0:T(8,128)(2,1)S(1)} %shard_map.74), channel_id=1, source_target_pairs={{0,64},{64,0},{1,65},{65,1},{2,66},{66,2},{3,67},{67,3},{4,68},{68... | collective-permute-start | bytes 6291464 | tf_op jit(solution)/shard_map/ppermute | solution.py:18
  52.3 4.2 %collective-permute-start.4 = (bf16[256,512]{1,0:T(8,128)(2,1)S(1)}, bf16[256,512]{1,0:T(8,128)(2,1)S(1)}, u32[]{:S(2)}, u32[]{:S(2)}) collective-permute-start(bf16[256,512]{1,0:T(8,128)(2,1)S(1)} %bitcast.48), channel_id=1, source_target_pairs={{0,32},{16,48},{32,0},{48,16},{1,33},{17,49},{33,1},{49,17},{2,34}... | collective-permute-start | bytes 786440 | tf_op jit(solution)/shard_map/ppermute | solution.py:18
  56.5 3.3 %collective-permute-start.6 = (bf16[256,512]{1,0:T(8,128)(2,1)S(1)}, bf16[256,512]{1,0:T(8,128)(2,1)S(1)}, u32[]{:S(2)}, u32[]{:S(2)}) collective-permute-start(bf16[256,512]{1,0:T(8,128)(2,1)S(1)} %bitcast.49), channel_id=1, source_target_pairs={{0,48},{16,0},{32,16},{48,32},{1,49},{17,1},{33,17},{49,33},{2,50}... | collective-permute-start | bytes 786440 | tf_op jit(solution)/shard_map/ppermute | solution.py:18
  59.8 2.6 %collective-permute-start.8 = (bf16[256,512]{1,0:T(8,128)(2,1)S(1)}, bf16[256,512]{1,0:T(8,128)(2,1)S(1)}, u32[]{:S(2)}, u32[]{:S(2)}) collective-permute-start(bf16[256,512]{1,0:T(8,128)(2,1)S(1)} %bitcast.50), channel_id=1, source_target_pairs={{0,16},{16,32},{32,48},{48,0},{1,17},{17,33},{33,49},{49,1},{2,18}... | collective-permute-start | bytes 786440 | tf_op jit(solution)/shard_map/ppermute | solution.py:18
  62.4 2.5 %collective-permute-done.4 = bf16[256,512]{1,0:T(8,128)(2,1)S(1)} collective-permute-done((bf16[256,512]{1,0:T(8,128)(2,1)S(1)}, bf16[256,512]{1,0:T(8,128)(2,1)S(1)}, u32[]{:S(2)}, u32[]{:S(2)}) %collective-permute-start.4) | collective-permute-done | bytes 262176 | tf_op jit(solution)/shard_map/ppermute | solution.py:18
  64.9 0.0 collective-permute-done.3
  65.0 0.0 copy-done
  65.0 0.0 copy-done.2
  65.0 2.0 %shard_map.75 = (bf16[8,4,128,512]{3,2,1,0:T(8,128)(2,1)S(1)}, bf16[2,128,512]{2,1,0:T(8,128)(2,1)S(1)}) custom-call(s32[8,8]{1,0:T(8,128)S(1)} %bitcast.57, bf16[4,128,512]{2,1,0:T(8,128)(2,1)S(1)} %bitcast.43, bf16[4,128,512]{2,1,0:T(8,128)(2,1)S(1)} %bitcast.45, bf16[4,128,512]{2,1,0:T(8,128)(2,1)S(1)} %bitcast.46, bf16[4,128,512]{2,1,0:T(8,128)(2,1)S(1)} %bitcast.47, ...), custom_call_target="tpu_custom_call" | custom-call | flops 536870912 | bytes 4194304 | tf_op jit(solution)/shard_map/pallas_call | solution.py:122
  67.0 3.1 %collective-permute-done.6 = bf16[256,512]{1,0:T(8,128)(2,1)S(1)} collective-permute-done((bf16[256,512]{1,0:T(8,128)(2,1)S(1)}, bf16[256,512]{1,0:T(8,128)(2,1)S(1)}, u32[]{:S(2)}, u32[]{:S(2)}) %collective-permute-start.6) | collective-permute-done | bytes 262176 | tf_op jit(solution)/shard_map/ppermute | solution.py:18
  70.1 1.7 %shard_map.76 = bf16[2,128,512]{2,1,0:T(8,128)(2,1)S(1)} custom-call(s32[8,8]{1,0:T(8,128)S(1)} %bitcast.58, bf16[8,4,128,512]{3,2,1,0:T(8,128)(2,1)S(1)} %get-tuple-element.16.kv, bf16[2,128,512]{2,1,0:T(8,128)(2,1)S(1)} %bitcast.53, s32[8,8,16,128]{3,2,1,0:T(8,128)S(1)} %bitcast.40), custom_call_target="tpu_custom_call" | custom-call | flops 536870912 | bytes 4194304 | tf_op jit(solution)/shard_map/pallas_call | solution.py:146
  71.8 2.5 %collective-permute-start.7 = (bf16[256,512]{1,0:T(8,128)(2,1)S(1)}, bf16[256,512]{1,0:T(8,128)(2,1)S(1)}, u32[]{:S(2)}, u32[]{:S(2)}) collective-permute-start(bf16[256,512]{1,0:T(8,128)(2,1)S(1)} %bitcast.55), channel_id=1, source_target_pairs={{0,16},{16,32},{32,48},{48,0},{1,17},{17,33},{33,49},{49,1},{2,18}... | collective-permute-start | bytes 786440 | tf_op jit(solution)/shard_map/ppermute | solution.py:18
  74.3 0.0 collective-permute-done.8
  74.3 1.7 %shard_map.77 = bf16[2,128,512]{2,1,0:T(8,128)(2,1)S(1)} custom-call(s32[8,8]{1,0:T(8,128)S(1)} %bitcast.59, bf16[8,4,128,512]{3,2,1,0:T(8,128)(2,1)S(1)} %get-tuple-element.16.kv, bf16[2,128,512]{2,1,0:T(8,128)(2,1)S(1)} %bitcast.52, s32[8,8,16,128]{3,2,1,0:T(8,128)S(1)} %bitcast.41), custom_call_target="tpu_custom_call" | custom-call | flops 536870912 | bytes 4194304 | tf_op jit(solution)/shard_map/pallas_call | solution.py:146
  76.1 3.3 %collective-permute-start.9 = (bf16[256,512]{1,0:T(8,128)(2,1)S(1)}, bf16[256,512]{1,0:T(8,128)(2,1)S(1)}, u32[]{:S(2)}, u32[]{:S(2)}) collective-permute-start(bf16[256,512]{1,0:T(8,128)(2,1)S(1)} %bitcast.56), channel_id=1, source_target_pairs={{0,48},{16,0},{32,16},{48,32},{1,49},{17,1},{33,17},{49,33},{2,50}... | collective-permute-start | bytes 786440 | tf_op jit(solution)/shard_map/ppermute | solution.py:18
  79.4 4.2 %collective-permute-start.5 = (bf16[256,512]{1,0:T(8,128)(2,1)S(1)}, bf16[256,512]{1,0:T(8,128)(2,1)S(1)}, u32[]{:S(2)}, u32[]{:S(2)}) collective-permute-start(bf16[256,512]{1,0:T(8,128)(2,1)S(1)} %bitcast.62), channel_id=1, source_target_pairs={{0,32},{16,48},{32,0},{48,16},{1,33},{17,49},{33,1},{49,17},{2,34}... | collective-permute-start | bytes 786440 | tf_op jit(solution)/shard_map/ppermute | solution.py:18
  83.6 1.8 %shard_map.78 = f32[2,128,512]{2,1,0:T(8,128)S(1)} custom-call(s32[8,8]{1,0:T(8,128)S(1)} %bitcast.60, bf16[8,4,128,512]{3,2,1,0:T(8,128)(2,1)S(1)} %get-tuple-element.16.kv, bf16[2,128,512]{2,1,0:T(8,128)(2,1)S(1)} %bitcast.51, s32[8,8,16,128]{3,2,1,0:T(8,128)S(1)} %bitcast.42), custom_call_target="tpu_custom_call" | custom-call | flops 536870912 | bytes 4194304 | tf_op jit(solution)/shard_map/pallas_call | solution.py:146
  85.4 0.0 copy-start.1
  85.4 0.0 copy-start.3
  85.4 0.0 collective-permute-done.7
  85.4 1.1 collective-permute-done.9
  86.5 6.8 %collective-permute-done.5 = bf16[256,512]{1,0:T(8,128)(2,1)S(1)} collective-permute-done((bf16[256,512]{1,0:T(8,128)(2,1)S(1)}, bf16[256,512]{1,0:T(8,128)(2,1)S(1)}, u32[]{:S(2)}, u32[]{:S(2)}) %collective-permute-start.5) | collective-permute-done | bytes 262176 | tf_op jit(solution)/shard_map/ppermute | solution.py:18
  93.3 0.9 fusion.1
  94.1 11.8 %all-to-all-start.1 = ((bf16[16,16,512]{2,1,0:T(8,128)(2,1)}), bf16[16,16,512]{2,1,0:T(8,128)(2,1)S(1)}, u32[]{:S(2)}, u32[]{:S(2)}) async-start(bf16[16,16,512]{2,1,0:T(8,128)(2,1)} %bitcast.20), calls=%async_computation.1 | async-start | bytes 524288 | tf_op jit(solution)/shard_map/all_to_all | solution.py:184
  105.9 0.0 copy-done.1
  105.9 0.0 copy-done.3
  105.9 0.2 shard_map.73
  106.1 17.5 %all-to-all-done.1 = bf16[16,16,512]{2,1,0:T(8,128)(2,1)S(1)} async-done(((bf16[16,16,512]{2,1,0:T(8,128)(2,1)}), bf16[16,16,512]{2,1,0:T(8,128)(2,1)S(1)}, u32[]{:S(2)}, u32[]{:S(2)}) %all-to-all-start.1) | async-done | bytes 262176 | tf_op jit(solution)/shard_map/all_to_all | solution.py:184
  123.6 0.1 fusion.2
  123.8 0.7 fusion.5
  (1 shorter events, 0.0 us)
Async XLA Ops:
  1.4 48.7 %all-to-all-start = ((bf16[16,16,512]{2,1,0:T(8,128)(2,1)}), bf16[16,16,512]{2,1,0:T(8,128)(2,1)S(1)}, u32[]{:S(2)}, u32[]{:S(2)}) async-start(bf16[16,16,512]{2,1,0:T(8,128)(2,1)} %broadcast_in_dim.7), calls=%async_computation | async-start | bytes 524288 | tf_op jit(solution)/shard_map/all_to_all | solution.py:165
  17.7 26.8 %collective-permute-start = (bf16[512,512]{1,0:T(8,128)(2,1)S(1)}, bf16[512,512]{1,0:T(8,128)(2,1)S(1)}, u32[]{:S(2)}, u32[]{:S(2)}) collective-permute-start(bf16[512,512]{1,0:T(8,128)(2,1)S(1)} %pad_maximum_fusion.refs_0_), channel_id=1, source_target_pairs={{0,384},{128,0},{256,128},{384,256},{1,385},{129,1},{257,129},{385... | collective-permute-start | bytes 1572872 | tf_op jit(solution)/shard_map/ppermute | solution.py:18
  22.4 22.2 %collective-permute-start.1 = (bf16[512,512]{1,0:T(8,128)(2,1)S(1)}, bf16[512,512]{1,0:T(8,128)(2,1)S(1)}, u32[]{:S(2)}, u32[]{:S(2)}) collective-permute-start(bf16[512,512]{1,0:T(8,128)(2,1)S(1)} %pad_maximum_fusion.refs_0_), channel_id=1, source_target_pairs={{0,256},{128,384},{256,0},{384,128},{1,257},{129,385},{257,1},{385... | collective-permute-start | bytes 1572872 | tf_op jit(solution)/shard_map/ppermute | solution.py:18
  25.1 25.0 %collective-permute-start.2 = (bf16[512,512]{1,0:T(8,128)(2,1)S(1)}, bf16[512,512]{1,0:T(8,128)(2,1)S(1)}, u32[]{:S(2)}, u32[]{:S(2)}) collective-permute-start(bf16[512,512]{1,0:T(8,128)(2,1)S(1)} %pad_maximum_fusion.refs_0_), channel_id=1, source_target_pairs={{0,128},{128,256},{256,384},{384,0},{1,129},{129,257},{257,385},{3... | collective-permute-start | bytes 1572872 | tf_op jit(solution)/shard_map/ppermute | solution.py:18
  50.1 14.8 %copy-start = (s32[1,1,8,8,16,128]{5,4,3,2,1,0:T(8,128)S(1)}, s32[1,1,8,8,16,128]{5,4,3,2,1,0:T(8,128)}, u32[]{:S(2)}) copy-start(s32[1,1,8,8,16,128]{5,4,3,2,1,0:T(8,128)} %param.11) | copy-start | bytes 1572868
  50.1 14.8 %copy-start.2 = (s32[1,1,8,8]{3,2,1,0:T(8,128)S(1)}, s32[1,1,8,8]{3,2,1,0:T(8,128)}, u32[]{:S(2)}) copy-start(s32[1,1,8,8]{3,2,1,0:T(8,128)} %param.10) | copy-start | bytes 772
  50.3 14.7 %collective-permute-start.3 = (bf16[4,512,512]{2,1,0:T(8,128)(2,1)S(1)}, bf16[4,512,512]{2,1,0:T(8,128)(2,1)S(1)}, u32[]{:S(2)}, u32[]{:S(2)}) collective-permute-start(bf16[4,512,512]{2,1,0:T(8,128)(2,1)S(1)} %shard_map.74), channel_id=1, source_target_pairs={{0,64},{64,0},{1,65},{65,1},{2,66},{66,2},{3,67},{67,3},{4,68},{68... | collective-permute-start | bytes 6291464 | tf_op jit(solution)/shard_map/ppermute | solution.py:18
  52.3 12.6 %collective-permute-start.4 = (bf16[256,512]{1,0:T(8,128)(2,1)S(1)}, bf16[256,512]{1,0:T(8,128)(2,1)S(1)}, u32[]{:S(2)}, u32[]{:S(2)}) collective-permute-start(bf16[256,512]{1,0:T(8,128)(2,1)S(1)} %bitcast.48), channel_id=1, source_target_pairs={{0,32},{16,48},{32,0},{48,16},{1,33},{17,49},{33,1},{49,17},{2,34}... | collective-permute-start | bytes 786440 | tf_op jit(solution)/shard_map/ppermute | solution.py:18
  56.5 13.5 %collective-permute-start.6 = (bf16[256,512]{1,0:T(8,128)(2,1)S(1)}, bf16[256,512]{1,0:T(8,128)(2,1)S(1)}, u32[]{:S(2)}, u32[]{:S(2)}) collective-permute-start(bf16[256,512]{1,0:T(8,128)(2,1)S(1)} %bitcast.49), channel_id=1, source_target_pairs={{0,48},{16,0},{32,16},{48,32},{1,49},{17,1},{33,17},{49,33},{2,50}... | collective-permute-start | bytes 786440 | tf_op jit(solution)/shard_map/ppermute | solution.py:18
  59.8 14.5 %collective-permute-start.8 = (bf16[256,512]{1,0:T(8,128)(2,1)S(1)}, bf16[256,512]{1,0:T(8,128)(2,1)S(1)}, u32[]{:S(2)}, u32[]{:S(2)}) collective-permute-start(bf16[256,512]{1,0:T(8,128)(2,1)S(1)} %bitcast.50), channel_id=1, source_target_pairs={{0,16},{16,32},{32,48},{48,0},{1,17},{17,33},{33,49},{49,1},{2,18}... | collective-permute-start | bytes 786440 | tf_op jit(solution)/shard_map/ppermute | solution.py:18
  71.8 13.6 %collective-permute-start.7 = (bf16[256,512]{1,0:T(8,128)(2,1)S(1)}, bf16[256,512]{1,0:T(8,128)(2,1)S(1)}, u32[]{:S(2)}, u32[]{:S(2)}) collective-permute-start(bf16[256,512]{1,0:T(8,128)(2,1)S(1)} %bitcast.55), channel_id=1, source_target_pairs={{0,16},{16,32},{32,48},{48,0},{1,17},{17,33},{33,49},{49,1},{2,18}... | collective-permute-start | bytes 786440 | tf_op jit(solution)/shard_map/ppermute | solution.py:18
  76.1 10.4 %collective-permute-start.9 = (bf16[256,512]{1,0:T(8,128)(2,1)S(1)}, bf16[256,512]{1,0:T(8,128)(2,1)S(1)}, u32[]{:S(2)}, u32[]{:S(2)}) collective-permute-start(bf16[256,512]{1,0:T(8,128)(2,1)S(1)} %bitcast.56), channel_id=1, source_target_pairs={{0,48},{16,0},{32,16},{48,32},{1,49},{17,1},{33,17},{49,33},{2,50}... | collective-permute-start | bytes 786440 | tf_op jit(solution)/shard_map/ppermute | solution.py:18
  79.4 13.8 %collective-permute-start.5 = (bf16[256,512]{1,0:T(8,128)(2,1)S(1)}, bf16[256,512]{1,0:T(8,128)(2,1)S(1)}, u32[]{:S(2)}, u32[]{:S(2)}) collective-permute-start(bf16[256,512]{1,0:T(8,128)(2,1)S(1)} %bitcast.62), channel_id=1, source_target_pairs={{0,32},{16,48},{32,0},{48,16},{1,33},{17,49},{33,1},{49,17},{2,34}... | collective-permute-start | bytes 786440 | tf_op jit(solution)/shard_map/ppermute | solution.py:18
  85.4 20.5 %copy-start.1 = (bf16[512,512]{1,0:T(8,128)(2,1)S(1)}, bf16[512,512]{1,0:T(8,128)(2,1)}, u32[]{:S(2)}) copy-start(bf16[512,512]{1,0:T(8,128)(2,1)} %w_ref.1) | copy-start | bytes 1572868
  85.4 20.5 %copy-start.3 = (bf16[1,16,512]{2,1,0:T(8,128)(2,1)S(1)}, bf16[1,16,512]{2,1,0:T(8,128)(2,1)}, u32[]{:S(2)}) copy-start(bf16[1,16,512]{2,1,0:T(8,128)(2,1)} %param.12) | copy-start | bytes 49156
  94.1 29.5 %all-to-all-start.1 = ((bf16[16,16,512]{2,1,0:T(8,128)(2,1)}), bf16[16,16,512]{2,1,0:T(8,128)(2,1)S(1)}, u32[]{:S(2)}, u32[]{:S(2)}) async-start(bf16[16,16,512]{2,1,0:T(8,128)(2,1)} %bitcast.20), calls=%async_computation.1 | async-start | bytes 524288 | tf_op jit(solution)/shard_map/all_to_all | solution.py:184
